TPU v7x, 32 devices: a whole 2x2x4 slice. The times are simulated.
32 devices in a mesh: wide: 8 (over z, y), narrow: 4 (over x, core).
Axes of the slice: x: 2, y: 2, z: 4, core: 2. Of those that a mesh axis runs over, the one named last changes fastest.
Arguments:
- tokens: bfloat16 [80, 1024, 768], P('wide', 'narrow'), may hold values from -12 to 12, as said below
- usable: int32 [80, 1024], P('wide', 'narrow'), may hold values from 0 to 1, as said below
- conv_weight: bfloat16 [2304, 384], P(('wide', 'narrow')), may hold values from -0.125 to 0.125
- point_weight: bfloat16 [768, 384], P(('wide', 'narrow')), may hold values from -0.3125 to 0.3125
- head_weight: bfloat16 [768, 5313], P(('wide', 'narrow')), may hold values from -0.21875 to 0.21875
- first_gain: float32 [768], replicated, may hold values from 0.1 to 1.9
- first_shift: float32 [768], replicated, may hold values from -3 to 3
- second_gain: float32 [384], replicated, may hold values from 0.1 to 1.9
- second_shift: float32 [384], replicated, may hold values from -3 to 3
- point_bias: float32 [768], replicated, may hold values from -2 to 2
- head_bias: float32 [5313], replicated, may hold values from -1 to 1
- cot_block: bfloat16 [80, 1024, 768], P('wide', 'narrow'), may hold values from -6 to 6
- cot_tracks: bfloat16 [80, 5313, 1024], P('wide', None, 'narrow'), may hold values from -6 to 6
Outputs:
- block_out: bfloat16 [80, 1024, 768], P('wide', 'narrow')
- tracks_out: bfloat16 [80, 5313, 1024], P('wide', None, 'narrow')
- grad_tokens: float32 [80, 1024, 768], P('wide', 'narrow')
- grad_conv: float32 [2304, 384], P(('wide', 'narrow'))
- grad_point: float32 [768, 384], P(('wide', 'narrow'))
- grad_head: float32 [768, 5313], P(('wide', 'narrow'))
- grad_first_gain: float32 [768], replicated
- grad_first_shift: float32 [768], replicated
- grad_second_gain: float32 [384], replicated
- grad_second_shift: float32 [384], replicated
- grad_point_bias: float32 [768], replicated
- grad_head_bias: float32 [5313], replicated
Inputs may be any that keep to these rules, and one draw needn't show every extreme that they name: 1 marks a usable bin. Blacklisted runs of 16 aligned bins and scattered unmappable bins are 0, with a blacklist rate that differs from window to window; the first bin of every window is usable. `tokens`: activations of order one whose scale grows along the bins and windows.
All inputs are finite; a program needn't handle non-finite values.
Results may differ from a plain program's by a relative error of at most 0.008.
Values may be sent and summed in bfloat16 or wider, within the bound.
No kernel may reach another device: no remote copies, remote signals or barrier semaphores. Data moves between devices by JAX's collectives and lax.ppermute only.
A program may use at most 256 MiB of HBM per device.

v0:
```python
import jax
import jax.numpy as jnp
from jax import lax
from jax.sharding import PartitionSpec as P

DILATION_STEP = 11
epsilon = 1e-05


def with_halo(shard, sides, width):
    for axis, dim in sides:
        count, length = (lax.axis_size(axis), shard.shape[dim])
        up = [(i, (i + 1) % count) for i in range(count - 1)]
        down = [(j, i) for i, j in up]
        last = lax.slice_in_dim(shard, length - width, length, axis=dim)
        first = lax.slice_in_dim(shard, 0, width, axis=dim)
        before = lax.ppermute(last, axis, up)
        after = lax.ppermute(first, axis, down)
        shard = jnp.concatenate([before, shard, after], axis=dim)
    return shard


def norm_stats(values, weight):
    totals, counted = lax.psum(
        (jnp.sum(values * weight, axis=(0, 1)), jnp.sum(weight)), ("wide", "narrow")
    )
    mean_value = totals / counted
    centred = values - mean_value
    spread = lax.psum(jnp.sum(weight * centred * centred, axis=(0, 1)), ("wide", "narrow"))
    variance = spread / counted
    return (mean_value, lax.rsqrt(variance + epsilon), counted)


def convolve(padded_input, convolution_kernel, local_bin_count):
    hidden_state = jnp.einsum(
        "ldo,ov->ldv",
        padded_input[:, 0:local_bin_count],
        convolution_kernel[0],
        preferred_element_type=jnp.float32,
    )
    for kernel_position in range(1, 3):
        hidden_state = hidden_state + jnp.einsum(
            "ldo,ov->ldv",
            padded_input[
                :,
                kernel_position * DILATION_STEP : kernel_position * DILATION_STEP + local_bin_count,
            ],
            convolution_kernel[kernel_position],
            preferred_element_type=jnp.float32,
        )
    return hidden_state


def gelu_back(preact, upstream):
    return jax.vjp(jax.nn.gelu, preact)[1](upstream)[0]


def norm_back(grad_inner, normed, scale_inv, gain, grad_gain, grad_shift, weight, counted):
    grad_normed = grad_inner * gain
    return scale_inv * (
        grad_normed - weight / counted * (gain * grad_shift + normed * gain * grad_gain)
    )


def shards(
    tokens,
    usable,
    conv_weight,
    point_weight,
    head_weight,
    first_gain,
    first_shift,
    second_gain,
    second_shift,
    point_bias,
    head_bias,
    cot_block,
    cot_tracks,
):
    local_bin_count = tokens.shape[1]
    weight = usable.astype(jnp.float32)[:, :, None]
    row_weight = usable.astype(jnp.float32)[:, None, :]
    source = tokens.astype(jnp.float32)
    conv_full, point_full = (
        lax.all_gather(conv_weight, ("wide", "narrow"), axis=0, tiled=True),
        lax.all_gather(point_weight, ("wide", "narrow"), axis=0, tiled=True),
    )
    first_mean, first_scale, counted = norm_stats(source, weight)
    first_normed = (source - first_mean) * first_scale
    first_inner = first_normed * first_gain + first_shift
    first_activated = jax.nn.gelu(first_inner).astype(jnp.bfloat16)
    padded_input = with_halo(first_activated, (("narrow", 1),), DILATION_STEP)
    convolution_kernel = conv_full.reshape(3, -1, conv_full.shape[1])
    hidden_state = convolve(padded_input, convolution_kernel, local_bin_count)
    second_mean, second_scale, counted_two = norm_stats(hidden_state, weight)
    second_normed = (hidden_state - second_mean) * second_scale
    second_inner = second_normed * second_gain + second_shift
    second_active = jax.nn.gelu(second_inner).astype(jnp.bfloat16)
    branch = (
        jnp.einsum("wbh,ch->wbc", second_active, point_full, preferred_element_type=jnp.float32)
        + point_bias
    )
    block = (source + branch).astype(jnp.bfloat16)
    window_part = block
    logits = jnp.einsum(
        "wbc,ct->wtb",
        window_part,
        lax.all_gather(head_weight, ("wide", "narrow"), axis=0, tiled=True),
        preferred_element_type=jnp.float32,
    )
    logits = logits + head_bias[None, :, None]
    tracks = jax.nn.softplus(logits).astype(jnp.bfloat16)
    grad_logits = (cot_tracks.astype(jnp.float32) * row_weight * jax.nn.sigmoid(logits)).astype(
        jnp.bfloat16
    )
    grad_block = jnp.einsum(
        "wtb,ct->wbc",
        grad_logits,
        lax.all_gather(head_weight, ("wide", "narrow"), axis=0, tiled=True),
        preferred_element_type=jnp.float32,
    )
    window_part = block
    grad_head = lax.psum_scatter(
        jnp.einsum("wbc,wtb->ct", window_part, grad_logits, preferred_element_type=jnp.float32),
        ("wide", "narrow"),
        scatter_dimension=0,
        tiled=True,
    )
    grad_summed = cot_block.astype(jnp.float32) * weight + grad_block
    grad_branch = grad_summed.astype(jnp.bfloat16)
    conv_full, point_full = (
        lax.all_gather(conv_weight, ("wide", "narrow"), axis=0, tiled=True),
        lax.all_gather(point_weight, ("wide", "narrow"), axis=0, tiled=True),
    )
    convolution_kernel = conv_full.reshape(3, -1, conv_full.shape[1])
    first_normed = (source - first_mean) * first_scale
    first_inner = first_normed * first_gain + first_shift
    hidden_state = convolve(padded_input, convolution_kernel, local_bin_count)
    second_normed = (hidden_state - second_mean) * second_scale
    second_inner = second_normed * second_gain + second_shift
    second_active = jax.nn.gelu(second_inner).astype(jnp.bfloat16)
    grad_point_local = jnp.einsum(
        "wbc,wbh->ch", grad_branch, second_active, preferred_element_type=jnp.float32
    )
    grad_second_active = jnp.einsum(
        "ldo,ov->ldv", grad_branch, point_full, preferred_element_type=jnp.float32
    )
    grad_second_inner = gelu_back(second_inner, grad_second_active)
    bias_point_local = jnp.sum(grad_branch.astype(jnp.float32), axis=(0, 1))
    bias_head_local = jnp.sum(grad_logits.astype(jnp.float32), axis=(0, 2))
    grad_second_gain, grad_second_shift, grad_point_bias, grad_head_bias = lax.psum(
        (
            jnp.sum(grad_second_inner * second_normed, axis=(0, 1)),
            jnp.sum(grad_second_inner, axis=(0, 1)),
            bias_point_local,
            bias_head_local,
        ),
        ("wide", "narrow"),
    )
    hidden_gradient = norm_back(
        grad_second_inner,
        second_normed,
        second_scale,
        second_gain,
        grad_second_gain,
        grad_second_shift,
        weight,
        counted,
    ).astype(jnp.bfloat16)
    padded_gradient = with_halo(hidden_gradient, (("narrow", 1),), DILATION_STEP)
    grad_first_active = jnp.einsum(
        "wbh,ch->wbc",
        padded_gradient[:, 2 * DILATION_STEP : 2 * DILATION_STEP + local_bin_count],
        convolution_kernel[0],
        preferred_element_type=jnp.float32,
    )
    for kernel_position in range(1, 3):
        start_offset = (2 - kernel_position) * DILATION_STEP
        grad_first_active = grad_first_active + jnp.einsum(
            "wbh,ch->wbc",
            padded_gradient[:, start_offset : start_offset + local_bin_count],
            convolution_kernel[kernel_position],
            preferred_element_type=jnp.float32,
        )
    grad_taps = [
        jnp.einsum(
            "wbc,wbh->ch",
            padded_input[
                :,
                kernel_position * DILATION_STEP : kernel_position * DILATION_STEP + local_bin_count,
            ],
            hidden_gradient,
            preferred_element_type=jnp.float32,
        )
        for kernel_position in range(3)
    ]
    grad_conv_local = jnp.concatenate(grad_taps, axis=0)
    grad_first_inner = gelu_back(first_inner, grad_first_active)
    grad_first_gain, grad_first_shift = lax.psum(
        (
            jnp.sum(grad_first_inner * first_normed, axis=(0, 1)),
            jnp.sum(grad_first_inner, axis=(0, 1)),
        ),
        ("wide", "narrow"),
    )
    grad_tokens = grad_summed + norm_back(
        grad_first_inner,
        first_normed,
        first_scale,
        first_gain,
        grad_first_gain,
        grad_first_shift,
        weight,
        counted,
    )
    grad_conv, grad_point = (
        lax.psum_scatter(grad_conv_local, ("wide", "narrow"), scatter_dimension=0, tiled=True),
        lax.psum_scatter(grad_point_local, ("wide", "narrow"), scatter_dimension=0, tiled=True),
    )
    return (
        block,
        tracks,
        grad_tokens,
        grad_conv,
        grad_point,
        grad_head,
        grad_first_gain,
        grad_first_shift,
        grad_second_gain,
        grad_second_shift,
        grad_point_bias,
        grad_head_bias,
    )


def solution(mesh):
    placed = (
        P("wide", "narrow", None),
        P("wide", "narrow"),
        P(("wide", "narrow"), None),
        P(("wide", "narrow"), None),
        P(("wide", "narrow"), None),
        P(),
        P(),
        P(),
        P(),
        P(),
        P(),
        P("wide", "narrow", None),
        P("wide", None, "narrow"),
    )
    return jax.shard_map(
        shards,
        mesh=mesh,
        in_specs=placed,
        out_specs=(
            P("wide", "narrow", None),
            P("wide", None, "narrow"),
            P("wide", "narrow", None),
            P(("wide", "narrow"), None),
            P(("wide", "narrow"), None),
            P(("wide", "narrow"), None),
            P(),
            P(),
            P(),
            P(),
            P(),
            P(),
        ),
        check_vma=False,
    )
```

profile of v0, /device:TPU:0, one launch (start us, length us, event | category | flops | bytes accessed | tf_op | source)
XLA Modules:
  0.0 800.7 jit_solution(4075093609060179027)
XLA Ops:
  7.2 0.7 all-gather.3.cloned.1.call-update
  8.0 0.7 all-gather.5.cloned.1.call-update
  8.7 0.7 convert_element_type.42
  9.4 1.3 convert_reduce_fusion.2
  10.8 3.0 fusion.36
  13.7 42.3 %all-reduce.4 = (f32[768]{0:T(1024)S(1)}, f32[]{:T(128)}) all-reduce(f32[768]{0:T(1024)S(1)} %fusion.36, f32[]{:T(128)} %convert_reduce_fusion.2), channel_id=1, replica_groups=mesh['wide'=8,'narrow'=4] {'wide','narrow'}, use_global_device_ids=true, to_apply=%region_1.0 | all-reduce | flops 769 | bytes 6152 | tf_op jit(solution)/shard_map/psum | solution.py:24
  56.0 0.6 broadcast_divide_fusion.1
  56.7 2.9 fusion.38
  59.6 40.8 %psum.82 = f32[768]{0:T(1024)S(1)} all-reduce(f32[768]{0:T(1024)S(1)} %fusion.38), channel_id=1, replica_groups=mesh['wide'=8,'narrow'=4] {'wide','narrow'}, use_global_device_ids=true, to_apply=%region_5.0 | all-reduce | flops 768 | bytes 6144 | tf_op jit(solution)/shard_map/psum | solution.py:29
  100.4 0.7 add_rsqrt_fusion
  101.1 5.4 fusion.24
  106.5 1.9 copy-done.1
  108.3 0.1 fusion.71
  108.4 1.3 collective-permute-start
  109.7 1.3 collective-permute-start.1
  111.0 1.3 broadcast_divide_fusion
  112.3 48.0 %all_gather.13 = bf16[768,384]{1,0:T(8,128)(2,1)S(1)} all-gather(bf16[24,384]{1,0:T(8,128)(2,1)S(1)} %copy-done.20), channel_id=1, replica_groups=mesh['wide'=8,'narrow'=4] {'wide','narrow'}, dimensions={0}, use_global_device_ids=true | all-gather | bytes 608256 | tf_op jit(solution)/shard_map/all_gather | solution.py:86
  160.3 4.7 fusion.60
  165.0 2.2 fusion.47
  167.3 4.1 multiply_reduce_fusion.1
  171.4 37.1 %psum.83 = f32[384]{0:T(512)S(1)} all-reduce(f32[384]{0:T(512)S(1)} %get-tuple-element.33), channel_id=1, replica_groups=mesh['wide'=8,'narrow'=4] {'wide','narrow'}, use_global_device_ids=true, to_apply=%region_7.0 | all-reduce | flops 384 | bytes 3072 | tf_op jit(solution)/shard_map/psum | solution.py:24
  208.5 0.6 broadcast_divide_fusion.2
  209.2 2.7 fusion.46
  211.8 41.1 %psum.84 = f32[384]{0:T(512)S(1)} all-reduce(f32[384]{0:T(512)S(1)} %fusion.46), channel_id=1, replica_groups=mesh['wide'=8,'narrow'=4] {'wide','narrow'}, use_global_device_ids=true, to_apply=%region_9.0 | all-reduce | flops 384 | bytes 3072 | tf_op jit(solution)/shard_map/psum | solution.py:29
  253.0 0.7 add_rsqrt_fusion.1
  253.7 8.8 %fusion.37 = bf16[10,256,768]{2,1,0:T(8,128)(2,1)} fusion(bf16[10,256,768]{2,1,0:T(8,128)(2,1)} %param.13, f32[768]{0:T(1024)S(1)} %copy-done.34, bf16[768,384]{1,0:T(8,128)(2,1)S(1)} %all_gather.13, f32[10,256,384]{2,1,0:T(8,128)} %get-tuple-element.34, f32[384]{0:T(512)S(1)} %copy-done.35, f32[384]{0:T(512)S(1)} %copy-done.21, ...), kind=kOutput, calls=%fused_computation.49 | convolution fusion | flops 1530593280 | bytes 12395520 | tf_op jit(solution)/shard_map/wbh,ch->wbc/dot_general | solution.py:100
  262.5 73.0 %convert_reduce_fusion = (f32[5313]{0:T(1024)S(1)}, bf16[10,5313,256]{2,1,0:T(8,128)(2,1)}, bf16[10,5313,256]{2,1,0:T(8,128)(2,1)}) fusion(f32[5313]{0:T(1024)S(1)} %copy-done.33, f32[10,256]{1,0:T(8,128)S(1)} %convert_element_type.42, bf16[10,5313,256]{2,1,0:T(8,128)(2,1)} %param.25, bf16[10,256,768]{2,1,0:T(8,128)(2,1)} %fusion.37, ...), kind=kOutput, calls=%fused_computation.13 | convolution fusion | flops 21122775040 | bytes 93753352 | tf_op jit(solution)/shard_map/wbc,ct->wtb/dot_general | solution.py:105
  335.6 41.4 %convert_reduce_fusion.1 = (f32[768]{0:T(1024)S(1)}, bf16[10,256,768]{2,1,0:T(8,128)(2,1)S(1)}, f32[10,256,768]{2,1,0:T(8,128)}) fusion(f32[10,256]{1,0:T(8,128)S(1)} %convert_element_type.42, bf16[10,256,768]{2,1,0:T(8,128)(2,1)} %param.24, bf16[10,5313,256]{2,1,0:T(8,128)(2,1)} %get-tuple-element.25, bf16[768,5313]{1,0:T(8,128)(2,1)} %all-gather.5.cloned.1.call-done), kind=kOutput, calls=%fused_computation.51 | convolution fusion | flops 20903362560 | bytes 51105280 | tf_op jit(solution)/shard_map/wtb,ct->wbc/dot_general | solution.py:116
  377.0 2.0 copy-done.37
  379.0 3.4 convolution_bitcast_fusion.1
  382.4 8.9 %fusion.68 = (f32[384]{0:T(512)S(1)}, f32[384]{0:T(512)S(1)}, f32[10,256,384]{2,1,0:T(8,128)}) fusion(f32[384]{0:T(512)S(1)} %copy-done.24, f32[10,256,384]{2,1,0:T(8,128)} %get-tuple-element.34, f32[384]{0:T(512)S(1)} %copy-done.19, f32[384]{0:T(512)S(1)} %copy-done.36, f32[384]{0:T(512)S(1)} %copy-done.22, bf16[10,256,768]{2,1,0:T(8,128)(2,1)} %copy-done.37, ...), kind=kOutput, calls=%fused_computation.108 | convolution fusion | flops 1535507712 | bytes 12395520 | tf_op jit(solution)/shard_map/ldo,ov->ldv/dot_general | solution.py:145
  391.3 39.6 %all-reduce.3 = (f32[384]{0:T(512)S(1)}, f32[384]{0:T(512)S(1)}) all-reduce(f32[384]{0:T(512)S(1)} %get-tuple-element.15, f32[384]{0:T(512)S(1)} %get-tuple-element.14), channel_id=1, replica_groups=mesh['wide'=8,'narrow'=4] {'wide','narrow'}, use_global_device_ids=true, to_apply=%region_13.14 | all-reduce | flops 768 | bytes 6144 | tf_op jit(solution)/shard_map/psum | solution.py:151
  430.9 4.1 multiply_convert_fusion
  435.1 0.2 copy-done.3
  435.4 2.2 fusion.55
  437.6 2.3 fusion.56
  439.9 2.2 convolution_bitcast_fusion.2
  442.1 2.1 pad_maximum_fusion.2
  444.3 29.4 %convolution_bitcast_fusion = f32[768,5313]{1,0:T(8,128)} fusion(bf16[10,256,768]{2,1,0:T(8,128)(2,1)} %fusion.37, bf16[10,5313,256]{2,1,0:T(8,128)(2,1)} %get-tuple-element.25), kind=kOutput, calls=%fused_computation.19 | convolution fusion | flops 20891566080 | bytes 47456256 | tf_op jit(solution)/shard_map/wbc,wtb->ct/dot_general | solution.py:124
  473.8 1.3 collective-permute-start.2
  475.1 3.0 collective-permute-start.3
  478.1 3.3 fusion.59
  481.5 3.5 fusion.53
  485.0 11.6 %fusion.67 = (f32[768]{0:T(1024)S(1)}, f32[768]{0:T(1024)S(1)}, f32[10,256,768]{2,1,0:T(8,128)}) fusion(f32[768]{0:T(1024)S(1)} %copy-done.17, f32[768]{0:T(1024)S(1)} %copy-done.13, bf16[10,256,768]{2,1,0:T(8,128)(2,1)S(1)} %copy-done, f32[768]{0:T(1024)S(1)} %copy-done.26, f32[768]{0:T(1024)S(1)} %copy-done.15, ...), kind=kOutput, calls=%fused_computation.107 | convolution fusion | flops 1570896384 | bytes 30183936 | tf_op jit(solution)/shard_map/wbh,ch->wbc/dot_general | solution.py:179
  496.6 41.1 %all-reduce.2 = (f32[768]{0:T(1024)S(1)}, f32[768]{0:T(1024)S(1)}, f32[768]{0:T(1024)}, f32[5313]{0:T(1024)}) all-reduce(f32[768]{0:T(1024)S(1)} %get-tuple-element.13, f32[768]{0:T(1024)S(1)} %get-tuple-element.12, f32[768]{0:T(1024)S(1)} %get-tuple-element.26, ...), channel_id=1, replica_groups=mesh['wide'=8,'narrow'=4] {'wide','narrow'}, use_global_device_ids=true, to_apply=%region_17.18 | all-reduce | flops 7617 | bytes 60936 | tf_op jit(solution)/shard_map/psum | solution.py:199
  537.7 13.5 %fusion.31 = f32[10,256,768]{2,1,0:T(8,128)} fusion(bf16[10,256,768]{2,1,0:T(8,128)(2,1)} %param.13, f32[10,256,768]{2,1,0:T(8,128)} %get-tuple-element.37, f32[10,256,768]{2,1,0:T(8,128)} %get-tuple-element.35, bf16[10,256,768]{2,1,0:T(8,128)(2,1)} %param.24, f32[768]{0:T(1024)S(1)} %get-tuple-element.16, f32[768]{0:T(1024)S(1)} %mul.333, ...), kind=kLoop, calls=%fused_computation.43 | loop fusion | flops 27525120 | bytes 31493120 | tf_op jit(solution)/shard_map/add | solution.py:206
  551.3 45.8 %reduce-scatter.10.cloned.1.call-done = f32[72,384]{1,0:T(8,128)} async-done(((f32[2304,384]{1,0:T(8,128)}), f32[72,384]{1,0:T(8,128)}) %reduce-scatter.10.cloned.1.call-update) | async-done | bytes 110608
  597.0 196.7 %reduce-scatter.8.cloned.1.call-done = f32[24,5313]{1,0:T(8,128)} async-done(((f32[768,5313]{1,0:T(8,128)}), f32[24,5313]{1,0:T(8,128)}) %reduce-scatter.8.cloned.1.call-update) | async-done | bytes 510064 | tf_op jit(solution)/shard_map/reduce_scatter | solution.py:123
  (91 shorter events, 0.5 us)
Async XLA Ops:
  7.2 153.1 %all-gather.3.cloned.1.call-start = ((), (), s32[]{:S(2)}) async-start(), calls=%async_computation.3 | async-start | bytes 1824768 | tf_op jit(solution)/shard_map/all_gather | solution.py:85
  7.9 254.6 %all-gather.5.cloned.1.call-start = ((), (), s32[]{:S(2)}) async-start(), calls=%async_computation.4 | async-start | bytes 8515584 | tf_op jit(solution)/shard_map/all_gather | solution.py:108
  8.7 542.6 %reduce-scatter.12.cloned.1.call-start = ((), (), s32[]{:S(2)}) async-start(), calls=%async_computation.7 | async-start | bytes 1216512
  10.8 90.3 %copy-start.14 = (f32[768]{0:T(1024)S(1)}, f32[768]{0:T(1024)}, u32[]{:S(2)}) copy-start(f32[768]{0:T(1024)} %param.18) | copy-start | bytes 9220
  10.8 90.3 %copy-start.25 = (f32[768]{0:T(1024)S(1)}, f32[768]{0:T(1024)}, u32[]{:S(2)}) copy-start(f32[768]{0:T(1024)} %param.19) | copy-start | bytes 9220
  56.7 49.8 %copy-start.12 = (f32[768]{0:T(1024)}, f32[768]{0:T(1024)S(1)}, u32[]{:S(2)}) copy-start(f32[768]{0:T(1024)S(1)} %broadcast_divide_fusion.1) | copy-start | bytes 9220
  101.0 5.4 copy-start.16
  101.1 10.0 %copy-start.11 = (s32[10,256]{1,0:T(8,128)S(1)}, s32[10,256]{1,0:T(8,128)}, u32[]{:S(2)}) copy-start(s32[10,256]{1,0:T(8,128)} %param.14) | copy-start | bytes 30724
  101.1 11.2 %copy-start.20 = (bf16[24,384]{1,0:T(8,128)(2,1)S(1)}, bf16[24,384]{1,0:T(8,128)(2,1)}, u32[]{:S(2)}) copy-start(bf16[24,384]{1,0:T(8,128)(2,1)} %param.16) | copy-start | bytes 55300
  106.5 1.9 copy-start.1
  108.4 56.6 %collective-permute-start = (bf16[10,11,768]{2,1,0:T(8,128)(2,1)S(1)}, bf16[10,11,768]{2,1,0:T(8,128)(2,1)S(1)}, u32[]{:S(2)}, u32[]{:S(2)}) collective-permute-start(bf16[10,11,768]{2,1,0:T(8,128)(2,1)S(1)} %get-tuple-element.30), channel_id=1, source_target_pairs={{0,1},{1,2},{2,3},{4,5},{5,6},{6,7},{8,9},{9,10},{10,11},{12,13},{... | collective-permute-start | bytes 506888 | tf_op jit(solution)/shard_map/ppermute | solution.py:17
  109.7 57.5 %collective-permute-start.1 = (bf16[10,11,768]{2,1,0:T(8,128)(2,1)S(1)}, bf16[10,11,768]{2,1,0:T(8,128)(2,1)S(1)}, u32[]{:S(2)}, u32[]{:S(2)}) collective-permute-start(bf16[10,11,768]{2,1,0:T(8,128)(2,1)S(1)} %get-tuple-element.29), channel_id=1, source_target_pairs={{1,0},{2,1},{3,2},{5,4},{6,5},{7,6},{9,8},{10,9},{11,10},{13,12},{... | collective-permute-start | bytes 506888 | tf_op jit(solution)/shard_map/ppermute | solution.py:18
  160.3 93.4 %copy-start.6 = (bf16[768,384]{1,0:T(8,128)(2,1)}, bf16[768,384]{1,0:T(8,128)(2,1)S(1)}, u32[]{:S(2)}) copy-start(bf16[768,384]{1,0:T(8,128)(2,1)S(1)} %all_gather.13) | copy-start | bytes 1769476
  160.3 4.7 copy-start.2
  160.3 4.7 copy-start.5
  165.0 2.2 copy-start.31
  167.3 4.1 copy-start.8
  171.4 82.3 %copy-start.21 = (f32[384]{0:T(512)S(1)}, f32[384]{0:T(512)}, u32[]{:S(2)}) copy-start(f32[384]{0:T(512)} %param.20) | copy-start | bytes 4612
  171.4 82.3 %copy-start.34 = (f32[768]{0:T(1024)S(1)}, f32[768]{0:T(1024)}, u32[]{:S(2)}) copy-start(f32[768]{0:T(1024)} %param.22) | copy-start | bytes 9220
  171.4 82.3 %copy-start.35 = (f32[384]{0:T(512)S(1)}, f32[384]{0:T(512)}, u32[]{:S(2)}) copy-start(f32[384]{0:T(512)} %param.21) | copy-start | bytes 4612
  209.2 53.4 %copy-start.18 = (f32[384]{0:T(512)}, f32[384]{0:T(512)S(1)}, u32[]{:S(2)}) copy-start(f32[384]{0:T(512)S(1)} %broadcast_divide_fusion.2) | copy-start | bytes 4612
  253.7 8.8 %copy-start.23 = (f32[384]{0:T(512)}, f32[384]{0:T(512)S(1)}, u32[]{:S(2)}) copy-start(f32[384]{0:T(512)S(1)} %add_rsqrt_fusion.1) | copy-start | bytes 4612
  253.7 8.8 %copy-start.33 = (f32[5313]{0:T(1024)S(1)}, f32[5313]{0:T(1024)}, u32[]{:S(2)}) copy-start(f32[5313]{0:T(1024)} %param.23) | copy-start | bytes 63760
  335.5 43.4 %copy-start.4 = (f32[10,256,384]{2,1,0:T(8,128)S(1)}, f32[10,256,384]{2,1,0:T(8,128)}, u32[]{:S(2)}) copy-start(f32[10,256,384]{2,1,0:T(8,128)} %get-tuple-element.34) | copy-start | bytes 11796484
  335.6 43.4 %copy-start.19 = (f32[384]{0:T(512)S(1)}, f32[384]{0:T(512)}, u32[]{:S(2)}) copy-start(f32[384]{0:T(512)} %copy-done.18) | copy-start | bytes 4612
  335.6 43.4 %copy-start.22 = (f32[384]{0:T(512)S(1)}, f32[384]{0:T(512)}, u32[]{:S(2)}) copy-start(f32[384]{0:T(512)} %param.20) | copy-start | bytes 4612
  335.6 43.4 %copy-start.24 = (f32[384]{0:T(512)S(1)}, f32[384]{0:T(512)}, u32[]{:S(2)}) copy-start(f32[384]{0:T(512)} %copy-done.23) | copy-start | bytes 4612
  335.6 43.4 %copy-start.36 = (f32[384]{0:T(512)S(1)}, f32[384]{0:T(512)}, u32[]{:S(2)}) copy-start(f32[384]{0:T(512)} %param.21) | copy-start | bytes 4612
  377.0 2.0 copy-start.37
  379.0 3.4 copy-start.7
  382.4 48.5 %copy-start.10 = (f32[10,256]{1,0:T(8,128)S(1)}, f32[10,256]{1,0:T(8,128)}, u32[]{:S(2)}) copy-start(f32[10,256]{1,0:T(8,128)} %broadcast_divide_fusion) | copy-start | bytes 30724
  391.3 205.8 %reduce-scatter.10.cloned.1.call-start = ((), (), s32[]{:S(2)}) async-start(), calls=%async_computation.6 | async-start | bytes 3649536
  430.9 4.2 copy-start.29
  430.9 4.2 copy-start.30
  430.9 4.4 copy-start.3
  430.9 4.4 copy-start.9
  435.4 2.2 copy-start.32
  444.2 349.5 %reduce-scatter.8.cloned.1.call-start = ((), (), s32[]{:S(2)}) async-start(), calls=%async_computation.5 | async-start | bytes 17031168 | tf_op jit(solution)/shard_map/reduce_scatter | solution.py:123
  473.8 7.7 collective-permute-start.2
  475.1 9.9 %collective-permute-start.3 = (bf16[10,11,384]{2,1,0:T(8,128)(2,1)S(1)}, bf16[10,11,384]{2,1,0:T(8,128)(2,1)S(1)}, u32[]{:S(2)}, u32[]{:S(2)}) collective-permute-start(bf16[10,11,384]{2,1,0:T(8,128)(2,1)S(1)} %get-tuple-element.31), channel_id=1, source_target_pairs={{0,1},{1,2},{2,3},{4,5},{5,6},{6,7},{8,9},{9,10},{10,11},{12,13},{... | collective-permute-start | bytes 253448 | tf_op jit(solution)/shard_map/ppermute | solution.py:17
  481.4 3.5 copy-start
  481.4 3.5 copy-start.13
  481.4 3.5 copy-start.15
  481.4 3.5 copy-start.17
  481.4 3.5 copy-start.26
  537.7 13.5 %copy-start.27 = (f32[768]{0:T(1024)}, f32[768]{0:T(1024)S(1)}, u32[]{:S(2)}) copy-start(f32[768]{0:T(1024)S(1)} %get-tuple-element.16) | copy-start | bytes 9220
  537.7 13.5 %copy-start.28 = (f32[768]{0:T(1024)}, f32[768]{0:T(1024)S(1)}, u32[]{:S(2)}) copy-start(f32[768]{0:T(1024)S(1)} %get-tuple-element.17) | copy-start | bytes 9220
Sparse Core Ops, SparseCore 0:
  10.8 58.2 all-gather.2
  72.0 79.8 all-gather.4
  391.4 97.2 reduce-scatter.11
  494.6 102.4 reduce-scatter.9
  603.8 189.8 reduce-scatter.7
where the time goes:
time: 810 us; the launch traced here: 801 us
  blocking collectives  290 us (36%)
  waiting for transfers between devices  244 us (30%)
  matrix products  201 us (25%)
  other arithmetic  39.6 us (5%)
  between operations  14.8 us (2%)
    reduce_scatter x1, waiting for transfers between devices, shards(): lax.psum_scatter(jnp.einsum('wbc,wtb->ct', window_part, grad_logits, pref...  197 us
    psum x2, blocking collectives, norm_stats(): lax.psum(jnp.sum(weight * centred * centred, axis=(0, 1)), ('wide', 'narr...  81.9 us
    psum x2, blocking collectives, norm_stats(): lax.psum((jnp.sum(values * weight, axis=(0, 1)), jnp.sum(weight)), ('wide...  79.4 us
    dot_general x1, matrix products, shards(): jnp.einsum('wbc,ct->wtb', window_part, lax.all_gather(head_weight, ('wide...  73 us
    all_gather x1, blocking collectives, shards(): lax.all_gather(point_weight, ('wide', 'narrow'), axis=0, tiled=True)  48 us
    unnamed x7, waiting for transfers between devices  47.2 us
    dot_general x1, matrix products, shards(): jnp.einsum('wtb,ct->wbc', grad_logits, lax.all_gather(head_weight, ('wide...  41.4 us
    psum x1, blocking collectives, shards(): lax.psum((jnp.sum(grad_first_inner * first_normed, axis=(0, 1)), jnp.sum(...  41.1 us
  transfers between devices with their start and end apart: 9, of which 2 were waited for; matrix products, arithmetic and copies ran while one was open for 14% of the time, Pallas kernels for 0%

commit v1 on v0

--- a/solution.py
+++ b/solution.py
@@ -2,9 +2,28 @@
 import jax.numpy as jnp
 from jax import lax
 from jax.sharding import PartitionSpec as P
+from jax.lax import axis_index, axis_size, ppermute
 
 DILATION_STEP = 11
 epsilon = 1e-05
+
+
+def lead_regions(dimension_no, x_part):
+    axis_key = ("wide", "narrow")
+    arr_next = axis_index(axis_key)
+    back = axis_size(axis_key)
+    outer, clean = (back, arr_next)
+    e_now, val2 = (x_part, 1)
+    while val2 < outer:
+        table = []
+        for rr in range(outer):
+            table.append((rr, rr ^ val2))
+        r2 = ppermute(e_now, axis_name=axis_key, perm=table)
+        front = jnp.concatenate([e_now, r2], dimension_no)
+        known = jnp.concatenate([r2, e_now], dimension_no)
+        e_now = jnp.where(clean & val2 == 0, front, known)
+        val2 = 2 * val2
+    return e_now
 
 
 def with_halo(shard, sides, width):
@@ -83,7 +102,7 @@
     source = tokens.astype(jnp.float32)
     conv_full, point_full = (
         lax.all_gather(conv_weight, ("wide", "narrow"), axis=0, tiled=True),
-        lax.all_gather(point_weight, ("wide", "narrow"), axis=0, tiled=True),
+        lead_regions(0, point_weight),
     )
     first_mean, first_scale, counted = norm_stats(source, weight)
     first_normed = (source - first_mean) * first_scale

time: 810 us -> 797 us (0.984)
  matrix products: 201 us -> 190 us
    dot_general x1, matrix products: 41.4 us -> 30.2 us  [shards(): jnp.einsum('wtb,ct->wbc', grad_logits, lax.all_gather(head_weight, ('wide...]
  transfers between devices with their start and end apart: 9 -> 14, of which waited for: 2 -> 3; matrix products, arithmetic and copies ran while one was open for 14% -> 16% of each run, Pallas kernels for 0% -> 0%
where the time goes in v1:
time: 797 us; the launch traced here: 791 us
  blocking collectives  288 us (36%)
  waiting for transfers between devices  241 us (30%)
  matrix products  190 us (24%)
  other arithmetic  40.6 us (5%)
  between operations  14.9 us (2%)
  starting transfers between devices  12 us (2%)
    reduce_scatter x1, waiting for transfers between devices, shards(): lax.psum_scatter(jnp.einsum('wbc,wtb->ct', window_part, grad_logits, pref...  197 us
    psum x2, blocking collectives, norm_stats(): lax.psum((jnp.sum(values * weight, axis=(0, 1)), jnp.sum(weight)), ('wide...  81.5 us
    psum x2, blocking collectives, norm_stats(): lax.psum(jnp.sum(weight * centred * centred, axis=(0, 1)), ('wide', 'narr...  79 us
    dot_general x1, matrix products, shards(): jnp.einsum('wbc,ct->wtb', window_part, lax.all_gather(head_weight, ('wide...  73.5 us
    all_gather x1, blocking collectives, shards(): lax.all_gather(point_weight, ('wide', 'narrow'), axis=0, tiled=True)  47.1 us
    psum x1, blocking collectives, shards(): lax.psum((jnp.sum(grad_second_inner * second_normed, axis=(0, 1)), jnp.su...  41.4 us
    unnamed x7, waiting for transfers between devices  39.8 us
    psum x1, blocking collectives, shards(): lax.psum((jnp.sum(grad_first_inner * first_normed, axis=(0, 1)), jnp.sum(...  39.3 us
  transfers between devices with their start and end apart: 14, of which 3 were waited for; matrix products, arithmetic and copies ran while one was open for 16% of the time, Pallas kernels for 0%

profile of v1, /device:TPU:0, one launch (start us, length us, event | category | flops | bytes accessed | tf_op | source)
XLA Modules:
  0.0 791.2 jit_solution(15318703242336893383)
XLA Ops:
  7.2 0.7 all-gather.3.cloned.1.call-update
  8.0 0.7 all-gather.5.cloned.1.call-update
  9.3 0.7 convert_element_type.42
  10.0 1.3 convert_reduce_fusion.2
  11.3 3.0 fusion.36
  14.3 41.8 %all-reduce.4 = (f32[768]{0:T(1024)S(1)}, f32[]{:T(128)}) all-reduce(f32[768]{0:T(1024)S(1)} %fusion.36, f32[]{:T(128)} %convert_reduce_fusion.2), channel_id=1, replica_groups=mesh['wide'=8,'narrow'=4] {'wide','narrow'}, use_global_device_ids=true, to_apply=%region_1.2 | all-reduce | flops 769 | bytes 6152 | tf_op jit(solution)/shard_map/psum | solution.py:43
  56.1 0.6 broadcast_divide_fusion.1
  56.7 2.9 fusion.38
  59.6 40.6 %psum.82 = f32[768]{0:T(1024)S(1)} all-reduce(f32[768]{0:T(1024)S(1)} %fusion.38), channel_id=1, replica_groups=mesh['wide'=8,'narrow'=4] {'wide','narrow'}, use_global_device_ids=true, to_apply=%region_5.6 | all-reduce | flops 768 | bytes 6144 | tf_op jit(solution)/shard_map/psum | solution.py:48
  100.3 0.7 add_rsqrt_fusion
  101.0 6.7 fusion.24
  107.7 2.5 collective-permute-start.3
  110.2 1.1 fusion.79
  111.4 1.3 collective-permute-start
  112.7 1.3 collective-permute-start.1
  114.0 1.7 collective-permute-start.4
  115.7 47.1 %all_gather.13 = bf16[768,384]{1,0:T(8,128)(2,1)} all-gather(bf16[24,384]{1,0:T(8,128)(2,1)S(1)} %copy-done.10), channel_id=1, replica_groups=mesh['wide'=8,'narrow'=4] {'wide','narrow'}, dimensions={0}, use_global_device_ids=true | all-gather | bytes 608256 | tf_op jit(solution)/shard_map/all_gather | solution.py:152
  162.9 1.3 broadcast_divide_fusion
  164.2 4.8 collective-permute-done.5
  169.2 4.6 fusion.67
  173.9 2.2 fusion.47
  176.1 4.1 multiply_reduce_fusion.1
  180.2 39.7 %psum.83 = f32[384]{0:T(512)S(1)} all-reduce(f32[384]{0:T(512)S(1)} %get-tuple-element.33), channel_id=1, replica_groups=mesh['wide'=8,'narrow'=4] {'wide','narrow'}, use_global_device_ids=true, to_apply=%region_7.8 | all-reduce | flops 384 | bytes 3072 | tf_op jit(solution)/shard_map/psum | solution.py:43
  220.6 2.7 fusion.46
  223.3 38.4 %psum.84 = f32[384]{0:T(512)S(1)} all-reduce(f32[384]{0:T(512)S(1)} %fusion.46), channel_id=1, replica_groups=mesh['wide'=8,'narrow'=4] {'wide','narrow'}, use_global_device_ids=true, to_apply=%region_9.10 | all-reduce | flops 384 | bytes 3072 | tf_op jit(solution)/shard_map/psum | solution.py:48
  261.8 0.7 add_rsqrt_fusion.1
  262.5 8.9 %fusion.37 = bf16[10,256,768]{2,1,0:T(8,128)(2,1)} fusion(bf16[10,256,768]{2,1,0:T(8,128)(2,1)} %param.13, f32[768]{0:T(1024)S(1)} %copy-done.32, bf16[384,384]{1,0:T(8,128)(2,1)S(1)} %collective-permute-done.6, bf16[384,384]{1,0:T(8,128)(2,1)S(1)} %maximum_select_fusion.1, pred[]{:T(512)S(6)} %eq.15, f32[10,256,384]{2,1,0:T(8,128)} %get-tuple-element.34, ...), kind=kOutput, calls=%fused_computation.49 | convolution fusion | flops 1533247488 | bytes 12395521 | tf_op jit(solution)/shard_map/wbh,ch->wbc/dot_general | solution.py:119
  271.4 73.5 %convert_reduce_fusion = (f32[5313]{0:T(1024)S(1)}, bf16[10,5313,256]{2,1,0:T(8,128)(2,1)}, bf16[10,5313,256]{2,1,0:T(8,128)(2,1)}) fusion(f32[5313]{0:T(1024)S(1)} %copy-done.31, f32[10,256]{1,0:T(8,128)S(1)} %convert_element_type.42, bf16[10,5313,256]{2,1,0:T(8,128)(2,1)} %param.25, bf16[10,256,768]{2,1,0:T(8,128)(2,1)} %fusion.37, ...), kind=kOutput, calls=%fused_computation.13 | convolution fusion | flops 21122775040 | bytes 93753352 | tf_op jit(solution)/shard_map/wbc,ct->wtb/dot_general | solution.py:124
  344.9 30.2 %convert_reduce_fusion.1 = (f32[768]{0:T(1024)S(1)}, bf16[10,256,768]{2,1,0:T(8,128)(2,1)S(1)}, f32[10,256,768]{2,1,0:T(8,128)}) fusion(f32[10,256]{1,0:T(8,128)S(1)} %convert_element_type.42, bf16[10,256,768]{2,1,0:T(8,128)(2,1)} %param.24, bf16[10,5313,256]{2,1,0:T(8,128)(2,1)} %get-tuple-element.25, bf16[768,5313]{1,0:T(8,128)(2,1)} %all-gather.5.cloned.1.call-done), kind=kOutput, calls=%fused_computation.51 | convolution fusion | flops 20903362560 | bytes 51105280 | tf_op jit(solution)/shard_map/wtb,ct->wbc/dot_general | solution.py:135
  375.1 2.0 copy-done.35
  377.1 3.4 convolution_bitcast_fusion.1
  380.6 8.9 %fusion.76 = (f32[384]{0:T(512)S(1)}, f32[384]{0:T(512)S(1)}, f32[10,256,384]{2,1,0:T(8,128)}) fusion(f32[384]{0:T(512)S(1)} %copy-done.22, f32[10,256,384]{2,1,0:T(8,128)} %get-tuple-element.34, f32[384]{0:T(512)S(1)} %copy-done.18, f32[384]{0:T(512)S(1)} %copy-done.34, f32[384]{0:T(512)S(1)} %copy-done.20, bf16[10,256,768]{2,1,0:T(8,128)(2,1)} %copy-done.35, ...), kind=kOutput, calls=%fused_computation.120 | convolution fusion | flops 1535507712 | bytes 12395520 | tf_op jit(solution)/shard_map/ldo,ov->ldv/dot_general | solution.py:164
  389.5 41.4 %all-reduce.3 = (f32[384]{0:T(512)S(1)}, f32[384]{0:T(512)S(1)}) all-reduce(f32[384]{0:T(512)S(1)} %get-tuple-element.15, f32[384]{0:T(512)S(1)} %get-tuple-element.14), channel_id=1, replica_groups=mesh['wide'=8,'narrow'=4] {'wide','narrow'}, use_global_device_ids=true, to_apply=%region_13.14 | all-reduce | flops 768 | bytes 6144 | tf_op jit(solution)/shard_map/psum | solution.py:170
  431.0 4.1 multiply_convert_fusion
  435.4 2.2 fusion.55
  437.7 2.3 fusion.56
  439.9 2.2 convolution_bitcast_fusion.2
  442.1 2.1 pad_maximum_fusion.2
  444.3 29.5 %convolution_bitcast_fusion = f32[768,5313]{1,0:T(8,128)} fusion(bf16[10,256,768]{2,1,0:T(8,128)(2,1)} %fusion.37, bf16[10,5313,256]{2,1,0:T(8,128)(2,1)} %get-tuple-element.25), kind=kOutput, calls=%fused_computation.19 | convolution fusion | flops 20891566080 | bytes 47456256 | tf_op jit(solution)/shard_map/wbc,wtb->ct/dot_general | solution.py:143
  473.9 1.3 collective-permute-start.7
  475.2 3.0 collective-permute-start.8
  478.2 3.3 fusion.66
  481.6 3.5 fusion.53
  485.1 11.6 %fusion.75 = (f32[768]{0:T(1024)S(1)}, f32[768]{0:T(1024)S(1)}, f32[10,256,768]{2,1,0:T(8,128)}) fusion(f32[768]{0:T(1024)S(1)} %copy-done.16, f32[768]{0:T(1024)S(1)} %copy-done.12, bf16[10,256,768]{2,1,0:T(8,128)(2,1)S(1)} %copy-done, f32[768]{0:T(1024)S(1)} %copy-done.24, f32[768]{0:T(1024)S(1)} %copy-done.14, ...), kind=kOutput, calls=%fused_computation.119 | convolution fusion | flops 1570896384 | bytes 30183936 | tf_op jit(solution)/shard_map/wbh,ch->wbc/dot_general | solution.py:198
  496.7 39.3 %all-reduce.2 = (f32[768]{0:T(1024)S(1)}, f32[768]{0:T(1024)S(1)}, f32[768]{0:T(1024)}, f32[5313]{0:T(1024)}) all-reduce(f32[768]{0:T(1024)S(1)} %get-tuple-element.13, f32[768]{0:T(1024)S(1)} %get-tuple-element.12, f32[768]{0:T(1024)S(1)} %get-tuple-element.26, ...), channel_id=1, replica_groups=mesh['wide'=8,'narrow'=4] {'wide','narrow'}, use_global_device_ids=true, to_apply=%region_17.18 | all-reduce | flops 7617 | bytes 60936 | tf_op jit(solution)/shard_map/psum | solution.py:218
  536.0 13.1 %fusion.31 = f32[10,256,768]{2,1,0:T(8,128)} fusion(bf16[10,256,768]{2,1,0:T(8,128)(2,1)} %param.13, f32[10,256,768]{2,1,0:T(8,128)} %get-tuple-element.37, f32[10,256,768]{2,1,0:T(8,128)} %get-tuple-element.35, bf16[10,256,768]{2,1,0:T(8,128)(2,1)} %param.24, f32[768]{0:T(1024)S(1)} %get-tuple-element.16, f32[768]{0:T(1024)S(1)} %mul.337, ...), kind=kLoop, calls=%fused_computation.43 | loop fusion | flops 27525120 | bytes 31493120 | tf_op jit(solution)/shard_map/add | solution.py:225
  549.2 38.4 %reduce-scatter.10.cloned.1.call-done = f32[72,384]{1,0:T(8,128)} async-done(((f32[2304,384]{1,0:T(8,128)}), f32[72,384]{1,0:T(8,128)}) %reduce-scatter.10.cloned.1.call-update) | async-done | bytes 110608
  587.5 196.6 %reduce-scatter.8.cloned.1.call-done = f32[24,5313]{1,0:T(8,128)} async-done(((f32[768,5313]{1,0:T(8,128)}), f32[24,5313]{1,0:T(8,128)}) %reduce-scatter.8.cloned.1.call-update) | async-done | bytes 510064 | tf_op jit(solution)/shard_map/reduce_scatter | solution.py:142
  (101 shorter events, 2.3 us)
Async XLA Ops:
  7.2 162.0 %all-gather.3.cloned.1.call-start = ((), (), s32[]{:S(2)}) async-start(), calls=%async_computation.3 | async-start | bytes 1824768 | tf_op jit(solution)/shard_map/all_gather | solution.py:104
  7.9 263.5 %all-gather.5.cloned.1.call-start = ((), (), s32[]{:S(2)}) async-start(), calls=%async_computation.4 | async-start | bytes 8515584 | tf_op jit(solution)/shard_map/all_gather | solution.py:127
  8.7 540.5 %reduce-scatter.12.cloned.1.call-start = ((), (), s32[]{:S(2)}) async-start(), calls=%async_computation.7 | async-start | bytes 1216512
  8.7 99.0 %collective-permute-start.2 = (bf16[24,384]{1,0:T(8,128)(2,1)}, bf16[24,384]{1,0:T(8,128)(2,1)S(1)}, u32[]{:S(2)}, u32[]{:S(2)}) collective-permute-start(bf16[24,384]{1,0:T(8,128)(2,1)} %param.16), channel_id=1, source_target_pairs={{0,1},{1,0},{2,3},{3,2},{4,5},{5,4},{6,7},{7,6},{8,9},{9,8},{10,11... | collective-permute-start | bytes 55304 | tf_op jit(solution)/shard_map/ppermute | solution.py:21
  11.3 89.6 %copy-start.13 = (f32[768]{0:T(1024)S(1)}, f32[768]{0:T(1024)}, u32[]{:S(2)}) copy-start(f32[768]{0:T(1024)} %param.18) | copy-start | bytes 9220
  11.3 89.6 %copy-start.23 = (f32[768]{0:T(1024)S(1)}, f32[768]{0:T(1024)}, u32[]{:S(2)}) copy-start(f32[768]{0:T(1024)} %param.19) | copy-start | bytes 9220
  56.7 51.0 %copy-start.11 = (f32[768]{0:T(1024)}, f32[768]{0:T(1024)S(1)}, u32[]{:S(2)}) copy-start(f32[768]{0:T(1024)S(1)} %broadcast_divide_fusion.1) | copy-start | bytes 9220
  100.9 6.7 copy-start.15
  100.9 6.7 copy-start.10
  101.0 62.0 %copy-start.9 = (s32[10,256]{1,0:T(8,128)S(1)}, s32[10,256]{1,0:T(8,128)}, u32[]{:S(2)}) copy-start(s32[10,256]{1,0:T(8,128)} %param.14) | copy-start | bytes 30724
  107.7 6.3 collective-permute-start.3
  111.4 62.5 %collective-permute-start = (bf16[10,11,768]{2,1,0:T(8,128)(2,1)S(1)}, bf16[10,11,768]{2,1,0:T(8,128)(2,1)S(1)}, u32[]{:S(2)}, u32[]{:S(2)}) collective-permute-start(bf16[10,11,768]{2,1,0:T(8,128)(2,1)S(1)} %get-tuple-element.30), channel_id=1, source_target_pairs={{0,1},{1,2},{2,3},{4,5},{5,6},{6,7},{8,9},{9,10},{10,11},{12,13},{... | collective-permute-start | bytes 506888 | tf_op jit(solution)/shard_map/ppermute | solution.py:36
  112.7 63.4 %collective-permute-start.1 = (bf16[10,11,768]{2,1,0:T(8,128)(2,1)S(1)}, bf16[10,11,768]{2,1,0:T(8,128)(2,1)S(1)}, u32[]{:S(2)}, u32[]{:S(2)}) collective-permute-start(bf16[10,11,768]{2,1,0:T(8,128)(2,1)S(1)} %get-tuple-element.29), channel_id=1, source_target_pairs={{1,0},{2,1},{3,2},{5,4},{6,5},{7,6},{9,8},{10,9},{11,10},{13,12},{... | collective-permute-start | bytes 506888 | tf_op jit(solution)/shard_map/ppermute | solution.py:37
  114.0 48.8 %collective-permute-start.4 = (bf16[96,384]{1,0:T(8,128)(2,1)S(1)}, bf16[96,384]{1,0:T(8,128)(2,1)S(1)}, u32[]{:S(2)}, u32[]{:S(2)}) collective-permute-start(bf16[96,384]{1,0:T(8,128)(2,1)S(1)} %maximum_select_fusion.3), channel_id=1, source_target_pairs={{0,4},{1,5},{2,6},{3,7},{4,0},{5,1},{6,2},{7,3},{8,12},{9,13},{10,... | collective-permute-start | bytes 221192 | tf_op jit(solution)/shard_map/ppermute | solution.py:21
  162.8 6.2 collective-permute-start.5
  169.1 93.3 %collective-permute-start.6 = (bf16[384,384]{1,0:T(8,128)(2,1)S(1)}, bf16[384,384]{1,0:T(8,128)(2,1)S(1)}, u32[]{:S(2)}, u32[]{:S(2)}) collective-permute-start(bf16[384,384]{1,0:T(8,128)(2,1)S(1)} %maximum_select_fusion.1), channel_id=1, source_target_pairs={{0,16},{1,17},{2,18},{3,19},{4,20},{5,21},{6,22},{7,23},{8,24},{9,... | collective-permute-start | bytes 884744 | tf_op jit(solution)/shard_map/ppermute | solution.py:21
  169.2 4.6 copy-start.1
  169.2 4.6 copy-start.4
  173.9 2.2 copy-start.29
  176.1 4.1 copy-start.6
  180.2 82.2 %copy-start.19 = (f32[384]{0:T(512)S(1)}, f32[384]{0:T(512)}, u32[]{:S(2)}) copy-start(f32[384]{0:T(512)} %param.20) | copy-start | bytes 4612
  180.2 82.2 %copy-start.32 = (f32[768]{0:T(1024)S(1)}, f32[768]{0:T(1024)}, u32[]{:S(2)}) copy-start(f32[768]{0:T(1024)} %param.22) | copy-start | bytes 9220
  180.2 82.2 %copy-start.33 = (f32[384]{0:T(512)S(1)}, f32[384]{0:T(512)}, u32[]{:S(2)}) copy-start(f32[384]{0:T(512)} %param.21) | copy-start | bytes 4612
  220.6 50.8 %copy-start.17 = (f32[384]{0:T(512)}, f32[384]{0:T(512)S(1)}, u32[]{:S(2)}) copy-start(f32[384]{0:T(512)S(1)} %broadcast_divide_fusion.2) | copy-start | bytes 4612
  262.4 9.0 %copy-start.21 = (f32[384]{0:T(512)}, f32[384]{0:T(512)S(1)}, u32[]{:S(2)}) copy-start(f32[384]{0:T(512)S(1)} %add_rsqrt_fusion.1) | copy-start | bytes 4612
  262.4 9.0 %copy-start.31 = (f32[5313]{0:T(1024)S(1)}, f32[5313]{0:T(1024)}, u32[]{:S(2)}) copy-start(f32[5313]{0:T(1024)} %param.23) | copy-start | bytes 63760
  344.9 32.2 %copy-start.3 = (f32[10,256,384]{2,1,0:T(8,128)S(1)}, f32[10,256,384]{2,1,0:T(8,128)}, u32[]{:S(2)}) copy-start(f32[10,256,384]{2,1,0:T(8,128)} %get-tuple-element.34) | copy-start | bytes 11796484
  344.9 32.2 %copy-start.18 = (f32[384]{0:T(512)S(1)}, f32[384]{0:T(512)}, u32[]{:S(2)}) copy-start(f32[384]{0:T(512)} %copy-done.17) | copy-start | bytes 4612
  344.9 32.2 %copy-start.20 = (f32[384]{0:T(512)S(1)}, f32[384]{0:T(512)}, u32[]{:S(2)}) copy-start(f32[384]{0:T(512)} %param.20) | copy-start | bytes 4612
  344.9 32.2 %copy-start.22 = (f32[384]{0:T(512)S(1)}, f32[384]{0:T(512)}, u32[]{:S(2)}) copy-start(f32[384]{0:T(512)} %copy-done.21) | copy-start | bytes 4612
  344.9 32.2 %copy-start.34 = (f32[384]{0:T(512)S(1)}, f32[384]{0:T(512)}, u32[]{:S(2)}) copy-start(f32[384]{0:T(512)} %param.21) | copy-start | bytes 4612
  377.1 3.5 copy-start.5
  380.6 50.4 %copy-start.8 = (f32[10,256]{1,0:T(8,128)S(1)}, f32[10,256]{1,0:T(8,128)}, u32[]{:S(2)}) copy-start(f32[10,256]{1,0:T(8,128)} %broadcast_divide_fusion) | copy-start | bytes 30724
  380.6 207.0 %reduce-scatter.10.cloned.1.call-start = ((), (), s32[]{:S(2)}) async-start(), calls=%async_computation.6 | async-start | bytes 3649536
  431.0 4.2 copy-start.27
  431.0 4.2 copy-start.28
  431.0 4.4 copy-start.2
  431.0 4.4 copy-start.7
  444.3 339.9 %reduce-scatter.8.cloned.1.call-start = ((), (), s32[]{:S(2)}) async-start(), calls=%async_computation.5 | async-start | bytes 17031168 | tf_op jit(solution)/shard_map/reduce_scatter | solution.py:142
  473.9 7.7 collective-permute-start.7
  475.2 9.9 %collective-permute-start.8 = (bf16[10,11,384]{2,1,0:T(8,128)(2,1)S(1)}, bf16[10,11,384]{2,1,0:T(8,128)(2,1)S(1)}, u32[]{:S(2)}, u32[]{:S(2)}) collective-permute-start(bf16[10,11,384]{2,1,0:T(8,128)(2,1)S(1)} %get-tuple-element.31), channel_id=1, source_target_pairs={{0,1},{1,2},{2,3},{4,5},{5,6},{6,7},{8,9},{9,10},{10,11},{12,13},{... | collective-permute-start | bytes 253448 | tf_op jit(solution)/shard_map/ppermute | solution.py:36
  481.5 3.5 copy-start
  481.5 3.5 copy-start.12
  481.5 3.5 copy-start.14
  481.5 3.5 copy-start.16
  481.6 3.5 copy-start.24
  536.0 13.1 %copy-start.25 = (f32[768]{0:T(1024)}, f32[768]{0:T(1024)S(1)}, u32[]{:S(2)}) copy-start(f32[768]{0:T(1024)S(1)} %get-tuple-element.16) | copy-start | bytes 9220
  536.0 13.1 %copy-start.26 = (f32[768]{0:T(1024)}, f32[768]{0:T(1024)S(1)}, u32[]{:S(2)}) copy-start(f32[768]{0:T(1024)S(1)} %get-tuple-element.17) | copy-start | bytes 9220
  (2 other events, 4.2 us)
Sparse Core Ops, SparseCore 0:
  10.8 58.2 all-gather.2
  72.0 79.8 all-gather.4
  380.7 98.3 reduce-scatter.11
  484.9 102.5 reduce-scatter.9
  594.3 189.8 reduce-scatter.7
